TPU v7x, 32 devices: a whole 2x2x4 slice. The times are simulated.
32 devices in a mesh: rep: 2 (over x), shard: 16 (over z, y, core).
Axes of the slice: x: 2, y: 2, z: 4, core: 2. Of those that a mesh axis runs over, the one named last changes fastest.
Arguments:
- tokens: bfloat16 [4096, 1024], P(('rep', 'shard')), may hold values from -6 to 6
- cotangent: bfloat16 [4096, 1024], P(('rep', 'shard')), may hold values from -6 to 6
- segment: int32 [4096], P(('rep', 'shard')), may hold values from -1 to 127, as said below
- params: float32 [12596224], P('shard'), as said below
- first_moment: float32 [12596224], P('shard'), may hold values from -6 to 6
- second_moment: float32 [12596224], P('shard'), may hold values from 0.01 to 1
Outputs:
- output_rows: bfloat16 [4096, 1024], P(('rep', 'shard'))
- input_grad: bfloat16 [4096, 1024], P(('rep', 'shard'))
- param_grad: float32 [12596224], P('shard')
- new_params: float32 [12596224], P('shard')
- new_first: float32 [12596224], P('shard')
- new_second: float32 [12596224], P('shard')
Inputs may be any that keep to these rules, and one draw needn't show every extreme that they name: `segment`: within each aligned block of 128 rows (the rows of one device) the occupied slots come first; an occupied slot holds the index within the block of the first slot of its sequence, so the first slot holds 0 and values never fall along the occupied slots; empty slots hold -1. `params`: the flat buffer in the layout of the steps.
All inputs are finite; a program needn't handle non-finite values.
Results may differ from a plain program's by a relative error of at most 0.023.
Values may be sent and summed in bfloat16 or wider, within the bound.
No kernel may reach another device: no remote copies, remote signals or barrier semaphores. Data moves between devices by JAX's collectives and lax.ppermute only.
A program may use at most 192 MiB of HBM per device.

v0:
```python
import math
import jax
import jax.numpy as jnp
from jax import lax
from jax.sharding import PartitionSpec as P

D = 1024
HEADS = 16
HD = 64
ROT = 16
FF = 4096
STEP = 4
norm_eps = 1e-05
adam_eps = 1e-08
beta_one = 0.9
beta_two = 0.999
learn_rate = 0.003
decay_rate = 0.1
root_half = 0.7071067811865476
inv_root_twopi = 0.3989422804014327


def extent_list():
    return [
        (D, 3 * D),
        (3 * D,),
        (D, D),
        (D,),
        (D, FF),
        (FF,),
        (FF, D),
        (D,),
        (D,),
        (D,),
        (D,),
        (D,),
    ]


def unpack(flat_vec):
    pieces = []
    offset = 0
    for extent in extent_list():
        amount = math.prod(extent)
        pieces.append(flat_vec[offset : offset + amount].reshape(extent))
        offset += amount
    return pieces


def norm_forward(residual, gain, shift):
    center = residual - jnp.mean(residual, axis=-1, keepdims=True)
    inverse = lax.rsqrt(jnp.mean(center * center, axis=-1, keepdims=True) + norm_eps)
    normed = center * inverse
    return (normed * gain + shift, normed, inverse)


def norm_backward(grad_norm, normed, inverse, gain):
    grad_hat = grad_norm * gain
    return inverse * (
        grad_hat
        - jnp.mean(grad_hat, axis=-1, keepdims=True)
        - normed * jnp.mean(grad_hat * normed, axis=-1, keepdims=True)
    )


def rotate(values, cosine, sine_part):
    half_rot = ROT // 2
    lower_half = values[..., :half_rot]
    upper_half = values[..., half_rot:ROT]
    return jnp.concatenate(
        [
            lower_half * cosine - upper_half * sine_part,
            upper_half * cosine + lower_half * sine_part,
            values[..., ROT:],
        ],
        axis=-1,
    )


def rotate_back(grads_in, cosine, sine_part):
    half_rot = ROT // 2
    lower_half = grads_in[..., :half_rot]
    upper_half = grads_in[..., half_rot:ROT]
    return jnp.concatenate(
        [
            lower_half * cosine + upper_half * sine_part,
            upper_half * cosine - lower_half * sine_part,
            grads_in[..., ROT:],
        ],
        axis=-1,
    )


def gelu_exact(values):
    return 0.5 * values * (1.0 + lax.erf(values * root_half))


def gelu_slope(values):
    return (
        0.5 * (1.0 + lax.erf(values * root_half))
        + values * jnp.exp(-0.5 * values * values) * inv_root_twopi
    )


def angles(segments):
    row_ids = jnp.arange(segments.shape[0], dtype=jnp.int32)
    position = (row_ids - segments).astype(jnp.float32)
    frequency = 10000.0 ** (-jnp.arange(0, ROT, 2, dtype=jnp.float32) / ROT)
    phases = position[:, None] * frequency[None, :]
    return (jnp.cos(phases)[:, None, :], jnp.sin(phases)[:, None, :])


def scores_of(queries, keys_bf, segments):
    raw = jnp.einsum("ihd,jhd->hij", queries, keys_bf, preferred_element_type=jnp.float32) * HD ** (
        -0.5
    )
    row_ids = jnp.arange(segments.shape[0], dtype=jnp.int32)
    allowed = (segments[:, None] == segments[None, :]) & (row_ids[None, :] <= row_ids[:, None])
    return jnp.where(allowed[None], raw, -1e30)


def layer_block(rows_in, rows_cot, segments, pieces):
    (
        w_qkv,
        b_qkv,
        w_out,
        b_out,
        w_up,
        b_up,
        w_down,
        b_down,
        gain_one,
        shift_one,
        gain_two,
        shift_two,
    ) = pieces
    length = rows_in.shape[0]
    residual = rows_in.astype(jnp.float32)
    normed_one, hat_one, inv_one = norm_forward(
        residual, gain_one.astype(jnp.float32), shift_one.astype(jnp.float32)
    )
    normed_two, hat_two, inv_two = norm_forward(
        residual, gain_two.astype(jnp.float32), shift_two.astype(jnp.float32)
    )
    input_one = normed_one.astype(jnp.bfloat16)
    input_two = normed_two.astype(jnp.bfloat16)
    mixed_rows = jnp.dot(input_one, w_qkv, preferred_element_type=jnp.float32) + b_qkv.astype(
        jnp.float32
    )
    cosine, sine_part = angles(segments)
    queries = rotate(mixed_rows[:, :D].reshape(length, HEADS, HD), cosine, sine_part).astype(
        jnp.bfloat16
    )
    keys_bf = rotate(mixed_rows[:, D : 2 * D].reshape(length, HEADS, HD), cosine, sine_part).astype(
        jnp.bfloat16
    )
    values_bf = mixed_rows[:, 2 * D :].reshape(length, HEADS, HD).astype(jnp.bfloat16)
    scores = scores_of(queries, keys_bf, segments)
    row_max = jnp.max(scores, axis=-1, keepdims=True)
    log_total = row_max + jnp.log(jnp.sum(jnp.exp(scores - row_max), axis=-1, keepdims=True))
    probs_bf = jnp.exp(scores - log_total).astype(jnp.bfloat16)
    heads_out = (
        jnp.einsum("hij,jhd->ihd", probs_bf, values_bf, preferred_element_type=jnp.float32)
        .reshape(length, D)
        .astype(jnp.bfloat16)
    )
    attention = jnp.dot(heads_out, w_out, preferred_element_type=jnp.float32) + b_out.astype(
        jnp.float32
    )
    hidden_pre = jnp.dot(input_two, w_up, preferred_element_type=jnp.float32) + b_up.astype(
        jnp.float32
    )
    active = gelu_exact(hidden_pre).astype(jnp.bfloat16)
    feed_out = jnp.dot(active, w_down, preferred_element_type=jnp.float32) + b_down.astype(
        jnp.float32
    )
    out_rows = (residual + attention + feed_out).astype(jnp.bfloat16)
    live_rows = (segments >= 0)[:, None]
    grad_bf = jnp.where(live_rows, rows_cot, jnp.zeros_like(rows_cot))
    grad_full = grad_bf.astype(jnp.float32)
    grad_w_down = jnp.dot(active.T, grad_bf, preferred_element_type=jnp.float32)
    grad_b_down = jnp.sum(grad_full, axis=0)
    grad_hidden = jnp.dot(grad_bf, w_down.T, preferred_element_type=jnp.float32) * gelu_slope(
        hidden_pre
    )
    grad_hidden_bf = grad_hidden.astype(jnp.bfloat16)
    grad_b_up = jnp.sum(grad_hidden, axis=0)
    grad_w_up = jnp.dot(input_two.T, grad_hidden_bf, preferred_element_type=jnp.float32)
    grad_norm_two = jnp.dot(grad_hidden_bf, w_up.T, preferred_element_type=jnp.float32)
    grad_w_out = jnp.dot(heads_out.T, grad_bf, preferred_element_type=jnp.float32)
    grad_heads = (
        jnp.dot(grad_bf, w_out.T, preferred_element_type=jnp.float32)
        .astype(jnp.bfloat16)
        .reshape(length, HEADS, HD)
    )
    delta_rows = jnp.einsum(
        "ihd,ihd->hi",
        grad_heads.astype(jnp.float32),
        heads_out.reshape(length, HEADS, HD).astype(jnp.float32),
    )
    probs_exact = jnp.exp(scores_of(queries, keys_bf, segments) - log_total)
    probs_again = probs_exact.astype(jnp.bfloat16)
    grad_values = jnp.einsum(
        "hij,ihd->jhd", probs_again, grad_heads, preferred_element_type=jnp.float32
    )
    grad_probs = jnp.einsum(
        "ihd,jhd->hij", grad_heads, values_bf, preferred_element_type=jnp.float32
    )
    grad_scores = (probs_exact * (grad_probs - delta_rows[:, :, None]) * HD ** (-0.5)).astype(
        jnp.bfloat16
    )
    grad_queries = jnp.einsum(
        "hij,jhd->ihd", grad_scores, keys_bf, preferred_element_type=jnp.float32
    )
    grad_keys = jnp.einsum("hij,ihd->jhd", grad_scores, queries, preferred_element_type=jnp.float32)
    grad_mixed = jnp.concatenate(
        [
            rotate_back(grad_queries, cosine, sine_part).reshape(length, D),
            rotate_back(grad_keys, cosine, sine_part).reshape(length, D),
            grad_values.reshape(length, D),
        ],
        axis=1,
    )
    grad_b_qkv = jnp.sum(grad_mixed, axis=0)
    grad_mixed_bf = grad_mixed.astype(jnp.bfloat16)
    grad_w_qkv = jnp.dot(input_one.T, grad_mixed_bf, preferred_element_type=jnp.float32)
    grad_norm_one = jnp.dot(grad_mixed_bf, w_qkv.T, preferred_element_type=jnp.float32)
    grad_rows = (
        grad_full
        + norm_backward(grad_norm_one, hat_one, inv_one, gain_one.astype(jnp.float32))
        + norm_backward(grad_norm_two, hat_two, inv_two, gain_two.astype(jnp.float32))
    ).astype(jnp.bfloat16)
    grad_list = [
        grad_w_qkv,
        grad_b_qkv,
        grad_w_out,
        grad_b_down,
        grad_w_up,
        grad_b_up,
        grad_w_down,
        grad_b_down,
        jnp.sum(grad_norm_one * hat_one, axis=0),
        jnp.sum(grad_norm_one, axis=0),
        jnp.sum(grad_norm_two * hat_two, axis=0),
        jnp.sum(grad_norm_two, axis=0),
    ]
    block_grad = jnp.concatenate([piece.reshape(-1).astype(jnp.bfloat16) for piece in grad_list])
    return (out_rows, grad_rows, block_grad)


def adam_update(weights, moment_one, moment_two, grad_total):
    first_new = beta_one * moment_one + (1.0 - beta_one) * grad_total
    second_new = beta_two * moment_two + (1.0 - beta_two) * grad_total * grad_total
    correct_one = 1.0 - beta_one**STEP
    correct_two = 1.0 - beta_two**STEP
    change = first_new / correct_one / (jnp.sqrt(second_new / correct_two) + adam_eps)
    return (weights - learn_rate * (change + decay_rate * weights), first_new, second_new)


def per_device(tokens, cotangent, segment, params, first_moment, second_moment):
    gathered = lax.all_gather(params.astype(jnp.bfloat16), "shard", axis=0, tiled=True)
    pieces = unpack(gathered)
    out_rows, grad_rows, block_grad = layer_block(tokens, cotangent, segment, pieces)
    owner_part = lax.psum_scatter(
        block_grad.astype(jnp.float32).astype(jnp.bfloat16),
        "shard",
        scatter_dimension=0,
        tiled=True,
    )
    grad_total = lax.psum(owner_part, "rep").astype(jnp.float32)
    new_weights, first_new, second_new = adam_update(
        params, first_moment, second_moment, grad_total
    )
    return (out_rows, grad_rows, grad_total, new_weights, first_new, second_new)


def solution(mesh):
    in_specs = (
        P(("rep", "shard"), None),
        P(("rep", "shard"), None),
        P(("rep", "shard")),
        P("shard"),
        P("shard"),
        P("shard"),
    )
    out_specs = (
        P(("rep", "shard"), None),
        P(("rep", "shard"), None),
        P("shard"),
        P("shard"),
        P("shard"),
        P("shard"),
    )
    return jax.shard_map(
        per_device, mesh=mesh, in_specs=in_specs, out_specs=out_specs, check_vma=False
    )
```

profile of v0, /device:TPU:0, one launch (start us, length us, event | category | flops | bytes accessed | tf_op | source)
XLA Modules:
  0.0 1133.9 jit_solution(3433474658904389262)
XLA Ops:
  7.2 2.0 convert_element_type.138
  10.6 8.5 broadcast.159
  19.0 24.7 %dynamic-update-slice = bf16[12596224]{0:T(1024)(128)(2,1)} dynamic-update-slice(bf16[12596224]{0:T(1024)(128)(2,1)} %broadcast.159, bf16[787264]{0:T(1024)(128)(2,1)S(1)} %convert_element_type.138, u32[]{:T(128)} %bitcast.2) | dynamic-update-slice | bytes 3149060
  45.4 438.3 %all-reduce.8.cloned.1.call-done = bf16[12596224]{0:T(1024)(128)(2,1)} async-done(((bf16[12596224]{0:T(1024)(128)(2,1)}), bf16[12596224]{0:T(1024)(128)(2,1)}) %all-reduce.8.cloned.1.call-update) | async-done | bytes 25192464
  483.7 6.4 slice.135
  490.1 10.3 reshape.206
  501.8 3.9 convolution_add_fusion.1
  507.5 2.3 slice.118
  509.8 2.5 convolution_convert_fusion
  515.9 4.6 convert_bitcast_fusion.2
  521.0 11.3 %fusion.61 = (bf16[4194304]{0:T(1024)(128)(2,1)}, bf16[4194304]{0:T(1024)(128)(2,1)}) fusion(bf16[12596224]{0:T(1024)(128)(2,1)} %all-reduce.8.cloned.1.call-done), kind=kLoop, calls=%fused_computation.130 | loop fusion | bytes 33554432 | tf_op jit(solution)/shard_map/slice | solution.py:45
  532.3 13.3 %slice.125 = bf16[4096,1024]{1,0:T(8,128)(2,1)} reshape(bf16[4194304]{0:T(1024)(128)(2,1)} %get-tuple-element.29) | data formatting | bytes 16777216 | tf_op jit(solution)/shard_map/slice | solution.py:45
  545.6 13.3 %reshape.209 = bf16[1024,4096]{1,0:T(8,128)(2,1)} reshape(bf16[4194304]{0:T(1024)(128)(2,1)} %get-tuple-element.28) | data formatting | bytes 16777216 | tf_op jit(solution)/shard_map/reshape | solution.py:45
  559.6 4.9 convolution_add_fusion
  565.4 3.5 fusion.65
  568.9 2.9 fusion.43
  571.8 5.7 convert_bitcast_fusion.1
  577.5 4.6 convert_bitcast_fusion
  582.2 3.2 fusion.38
  585.3 1.9 copy.59
  587.3 3.0 constant_dynamic-update-slice_fusion.9
  591.7 9.4 copy.61
  601.1 8.8 copy.62
  610.5 1.5 constant_dynamic-update-slice_fusion.8
  612.5 8.0 constant_dynamic-update-slice_fusion.6
  621.1 3.6 constant_dynamic-update-slice_fusion.5
  628.3 435.9 %all-reduce.10.cloned.1.call-done = bf16[12596224]{0:T(1024)(128)(2,1)} async-done(((bf16[12596224]{0:T(1024)(128)(2,1)}), bf16[12596224]{0:T(1024)(128)(2,1)}) %all-reduce.10.cloned.1.call-update) | async-done | bytes 25192464
  1064.2 3.4 dynamic-slice.2
  1067.7 2.1 fusion.34
  1069.8 5.3 convolution_add_fusion.3
  1076.3 42.7 %all-reduce.6.cloned.1.call-done = bf16[787264]{0:T(1024)(128)(2,1)} async-done(((bf16[787264]{0:T(1024)(128)(2,1)}), bf16[787264]{0:T(1024)(128)(2,1)}) %all-reduce.6.cloned.1.call-update) | async-done | bytes 1574544 | tf_op jit(solution)/shard_map/psum | solution.py:270
  1119.0 8.4 multiply_subtract_fusion
  (105 shorter events, 18.3 us)
Async XLA Ops:
  7.2 2.1 copy-start.12
  7.2 476.5 %all-reduce.8.cloned.1.call-start = ((), (), s32[]{:S(2)}) async-start(), calls=%async_computation.1 | async-start | bytes 50384896
  43.7 0.9 copy-start.1
  43.7 1.3 copy-start.11
  43.7 1.3 copy-start.3
  43.7 1020.5 %all-reduce.10.cloned.1.call-start = ((), (), s32[]{:S(2)}) async-start(), calls=%async_computation.2 | async-start | bytes 50384896
  505.7 1.8 slice-start.6
  509.8 2.8 copy-start.10
  515.9 4.6 copy-start.4
  515.9 4.6 copy-start.6
  559.6 5.8 copy-start
  559.6 9.2 slice-start
  565.4 3.5 slice-start.1
  571.8 10.4 copy-start.8
  571.8 10.4 slice-start.2
  571.8 13.5 %slice-start.7 = ((s8[6291456]{0:T(1024)(128)(4,1)}), s8[4194304]{0:T(1024)(128)(4,1)S(1)}, s32[]{:S(2)}) async-start(s8[6291456]{0:T(1024)(128)(4,1)} %bitcast.64), calls=%async_computation.10 | async-start | bytes 8388608
  577.5 4.7 slice-start.3
  577.5 4.7 copy-start.5
  577.5 4.7 copy-start.7
  577.5 7.8 slice-start.8
  612.5 8.6 slice-start.4
  612.5 8.6 slice-start.5
  627.5 440.1 %copy-start.9 = (f32[128,1024]{1,0:T(8,128)S(1)}, f32[128,1024]{1,0:T(8,128)}, u32[]{:S(2)}) copy-start(f32[128,1024]{1,0:T(8,128)} %copy-done.8) | copy-start | bytes 1572868
  627.6 491.5 %all-reduce.6.cloned.1.call-start = ((), (), s32[]{:S(2)}) async-start(), calls=%async_computation | async-start | bytes 3149824 | tf_op jit(solution)/shard_map/psum | solution.py:270
  1069.8 5.3 copy-start.2
Sparse Core Ops, SparseCore 0:
  43.9 439.7 all-reduce.7
  627.7 436.5 all-reduce.9
  1067.8 51.1 all-reduce.5
where the time goes:
time: 1140 us; the launch traced here: 1130 us
  waiting for transfers between devices  917 us (80%)
  local copies, waits for them, and re-layouts  140 us (12%)
  matrix products  45.2 us (4%)
  other arithmetic  16.2 us (1%)
  between operations  15.6 us (1%)
    unnamed x5, waiting for transfers between devices  874 us
    unnamed x61, local copies, waits for them, and re-layouts  79.8 us
    psum x1, waiting for transfers between devices, per_device(): grad_total = lax.psum(owner_part, 'rep').astype(jnp.float32)  42.7 us
    slice x6, local copies, waits for them, and re-layouts, unpack(): pieces.append(flat_vec[offset:offset + amount].reshape(extent))  34.2 us
    reshape x2, local copies, waits for them, and re-layouts, unpack(): pieces.append(flat_vec[offset:offset + amount].reshape(extent))  23.6 us
  transfers between devices with their start and end apart: 3, of which 3 were waited for; matrix products, arithmetic and copies ran while one was open for 1% of the time, Pallas kernels for 0%

commit v1 on v0

--- a/solution.py
+++ b/solution.py
@@ -267,7 +267,7 @@
         scatter_dimension=0,
         tiled=True,
     )
-    grad_total = lax.psum(owner_part, "rep").astype(jnp.float32)
+    grad_total = lax.all_gather(owner_part, "rep").sum(axis=0).astype(jnp.float32)
     new_weights, first_new, second_new = adam_update(
         params, first_moment, second_moment, grad_total
     )

time: 1140 us -> 1260 us (1.11)
  local copies, waits for them, and re-layouts: 140 us -> 176 us
  other arithmetic: 16.2 us -> 48.6 us
  waiting for transfers between devices: 917 us -> 949 us
    unnamed x5 -> x6, waiting for transfers between devices: 874 us -> 949 us
    psum x1 -> x0, waiting for transfers between devices: 42.7 us -> none  [per_device(): grad_total = lax.psum(owner_part, 'rep').astype(jnp.float32)]
    reduce_sum x0 -> x1, other arithmetic: none -> 32.9 us  [per_device(): lax.all_gather(owner_part, 'rep').sum(axis=0).astype(jnp.float32)]
    unnamed x61 -> x68, local copies, waits for them, and re-layouts: 79.8 us -> 108 us
where the time goes in v1:
time: 1260 us; the launch traced here: 1250 us
  waiting for transfers between devices  949 us (75%)
  local copies, waits for them, and re-layouts  176 us (14%)
  matrix products  56.2 us (4%)
  other arithmetic  48.6 us (4%)
  between operations  16.6 us (1%)
    unnamed x6, waiting for transfers between devices  949 us
    unnamed x68, local copies, waits for them, and re-layouts  108 us
    slice x6, local copies, waits for them, and re-layouts, unpack(): pieces.append(flat_vec[offset:offset + amount].reshape(extent))  34.2 us
    reduce_sum x1, other arithmetic, per_device(): lax.all_gather(owner_part, 'rep').sum(axis=0).astype(jnp.float32)  32.9 us
  transfers between devices with their start and end apart: 3, of which 3 were waited for; matrix products, arithmetic and copies ran while one was open for 1% of the time, Pallas kernels for 0%

profile of v1, /device:TPU:0, one launch (start us, length us, event | category | flops | bytes accessed | tf_op | source)
XLA Modules:
  0.0 1246.4 jit_solution(8914739560040263521)
XLA Ops:
  10.6 8.4 broadcast.159
  19.0 24.7 %dynamic-update-slice = bf16[12596224]{0:T(1024)(128)(2,1)} dynamic-update-slice(bf16[12596224]{0:T(1024)(128)(2,1)} %broadcast.159, bf16[787264]{0:T(1024)(128)(2,1)S(1)} %convert_element_type.140, u32[]{:T(128)} %bitcast.2) | dynamic-update-slice | bytes 3149060
  45.3 438.3 %all-reduce.7.cloned.1.call-done = bf16[12596224]{0:T(1024)(128)(2,1)} async-done(((bf16[12596224]{0:T(1024)(128)(2,1)}), bf16[12596224]{0:T(1024)(128)(2,1)}) %all-reduce.7.cloned.1.call-update) | async-done | bytes 25192464
  483.6 6.4 slice.135
  490.0 10.3 reshape.206
  501.7 3.9 convolution_add_fusion.1
  507.4 2.3 slice.118
  509.7 2.5 convolution_convert_fusion
  515.8 4.5 convert_bitcast_fusion.2
  520.8 11.3 fusion.61
  532.2 13.3 %slice.125 = bf16[4096,1024]{1,0:T(8,128)(2,1)} reshape(bf16[4194304]{0:T(1024)(128)(2,1)} %get-tuple-element.29) | data formatting | bytes 16777216 | tf_op jit(solution)/shard_map/slice | solution.py:45
  545.5 13.3 %reshape.209 = bf16[1024,4096]{1,0:T(8,128)(2,1)} reshape(bf16[4194304]{0:T(1024)(128)(2,1)} %get-tuple-element.28) | data formatting | bytes 16777216 | tf_op jit(solution)/shard_map/reshape | solution.py:45
  559.5 4.9 convolution_add_fusion
  565.2 14.1 %fusion.65 = (bf16[4096]{0:T(1024)(128)(2,1)S(1)}, bf16[128,4096]{1,0:T(8,128)(2,1)S(1)}) fusion(f32[128,4096]{1,0:T(8,128)S(1)} %convolution_add_fusion, bf16[4096,1024]{1,0:T(8,128)(2,1)S(1)} %copy-done, bf16[128,1024]{1,0:T(8,128)(2,1)S(1)} %copy-done.4, pred[128]{0:T(512)(128)(4,1)S(1)} %broadcast_compare_fusion), kind=kOutput, calls=%fused_computation.134 | convolution fusion | flops 1079635968 | bytes 11804800 | tf_op jit(solution)/shard_map/dot_general | solution.py:183
  579.4 2.9 fusion.43
  582.3 5.7 convert_bitcast_fusion.1
  588.0 4.7 convert_bitcast_fusion
  592.7 3.2 fusion.38
  597.9 3.0 constant_dynamic-update-slice_fusion.9
  602.3 9.4 copy.70
  611.7 8.8 copy.71
  623.1 8.1 constant_dynamic-update-slice_fusion.6
  631.8 3.6 constant_dynamic-update-slice_fusion.5
  640.8 434.2 %all-reduce.11.cloned.1.call-done = bf16[12596224]{0:T(1024)(128)(2,1)} async-done(((bf16[12596224]{0:T(1024)(128)(2,1)}), bf16[12596224]{0:T(1024)(128)(2,1)}) %all-reduce.11.cloned.1.call-update) | async-done | bytes 25192464
  1075.0 3.4 dynamic-slice.3
  1080.1 25.3 %dynamic-update-slice.1 = bf16[1574528]{0:T(1024)(128)(2,1)} dynamic-update-slice(bf16[1574528]{0:T(1024)(128)(2,1)} %broadcast.160, bf16[787264]{0:T(1024)(128)(2,1)} %dynamic-slice.3, u32[]{:T(128)} %bitcast.19) | dynamic-update-slice | bytes 3149060
  1105.6 2.1 fusion.34
  1107.7 5.6 convolution_add_fusion.3
  1114.5 76.6 %all-reduce.9.cloned.1.call-done = bf16[1574528]{0:T(1024)(128)(2,1)} async-done(((bf16[1574528]{0:T(1024)(128)(2,1)}), bf16[1574528]{0:T(1024)(128)(2,1)}) %all-reduce.9.cloned.1.call-update) | async-done | bytes 3149072
  1191.1 7.6 reshape.214
  1198.7 32.9 %reduce_sum.163 = bf16[787264]{0:T(1024)(128)(2,1)} reduce(bf16[2,787264]{1,0:T(2,128)(2,1)} %reshape.214, bf16[]{:T(256)} %constant.48.clone.1), dimensions={0}, to_apply=%region_16.17 | reduce | flops 787264 | bytes 4723586 | tf_op jit(solution)/shard_map/reduce_sum | solution.py:270
  1231.6 7.9 multiply_subtract_fusion
  (114 shorter events, 26.7 us)
Async XLA Ops:
  7.2 2.1 copy-start.13
  7.2 476.4 %all-reduce.7.cloned.1.call-start = ((), (), s32[]{:S(2)}) async-start(), calls=%async_computation | async-start | bytes 50384896
  43.6 0.9 copy-start.1
  43.6 1.3 copy-start.12
  43.7 1.3 copy-start.4
  43.7 1031.3 %all-reduce.11.cloned.1.call-start = ((), (), s32[]{:S(2)}) async-start(), calls=%async_computation.2 | async-start | bytes 50384896
  505.6 1.8 slice-start.6
  509.7 2.8 copy-start.11
  515.8 4.6 copy-start.5
  515.8 4.6 copy-start.7
  559.5 5.8 copy-start
  559.5 19.9 %slice-start = ((s8[8388608]{0:T(1024)(128)(4,1)}), s8[4194304]{0:T(1024)(128)(4,1)S(1)}, s32[]{:S(2)}) async-start(s8[8388608]{0:T(1024)(128)(4,1)} %bitcast.57), calls=%async_computation.3 | async-start | bytes 8388608
  565.2 14.1 %slice-start.1 = ((s8[8388608]{0:T(1024)(128)(4,1)}), s8[4194304]{0:T(1024)(128)(4,1)S(1)}, s32[]{:S(2)}) async-start(s8[8388608]{0:T(1024)(128)(4,1)} %bitcast.57), calls=%async_computation.4 | async-start | bytes 8388608
  582.3 10.5 copy-start.9
  582.3 10.4 slice-start.2
  582.3 13.7 %slice-start.7 = ((s8[6291456]{0:T(1024)(128)(4,1)}), s8[4194304]{0:T(1024)(128)(4,1)S(1)}, s32[]{:S(2)}) async-start(s8[6291456]{0:T(1024)(128)(4,1)} %bitcast.65), calls=%async_computation.10 | async-start | bytes 8388608
  588.0 4.7 slice-start.3
  588.0 4.7 copy-start.6
  588.0 4.7 copy-start.8
  588.0 7.9 slice-start.8
  623.1 8.7 slice-start.4
  623.1 8.7 slice-start.5
  638.2 0.7 copy-start.14
  638.3 552.8 %all-reduce.9.cloned.1.call-start = ((), (), s32[]{:S(2)}) async-start(), calls=%async_computation.1 | async-start | bytes 6299648
  1080.1 25.4 %copy-start.10 = (f32[128,1024]{1,0:T(8,128)S(1)}, f32[128,1024]{1,0:T(8,128)}, u32[]{:S(2)}) copy-start(f32[128,1024]{1,0:T(8,128)} %copy-done.9) | copy-start | bytes 1572868
  1107.7 5.6 copy-start.2
  1198.7 32.9 %copy-start.3 = (f32[787264]{0:T(1024)S(1)}, f32[787264]{0:T(1024)}, u32[]{:S(2)}) copy-start(f32[787264]{0:T(1024)} %param.9) | copy-start | bytes 9447172
Sparse Core Ops, SparseCore 0:
  43.8 439.7 all-reduce.6
  638.4 436.5 all-reduce.10
  1105.6 85.4 all-reduce.8
